TPU v7x, 32 devices: a whole 2x2x4 slice. The times are simulated.
32 devices in a mesh: mem: 8 (over z, x), head: 4 (over y, core).
Axes of the slice: x: 2, y: 2, z: 4, core: 2. Of those that a mesh axis runs over, the one named last changes fastest.
Arguments:
- tokens: bfloat16 [8192, 4096], P('mem'), may hold values from -14 to 14
- w_query: bfloat16 [4096, 4096], P(None, 'head'), may hold values from -0.09375 to 0.09375
- w_key: bfloat16 [4096, 1024], P(None, 'head'), may hold values from -0.09375 to 0.09375
- w_value: bfloat16 [4096, 1024], P(None, 'head'), may hold values from -0.09375 to 0.09375
- w_out: bfloat16 [4096, 4096], P('head'), may hold values from -0.09375 to 0.09375
- gate_bias: float32 [32], P('head'), may hold values from -4 to 4
- mem_keys: bfloat16 [65536, 1024], P('mem', 'head'), may hold values from -72 to 72
- mem_values: bfloat16 [65536, 1024], P('mem', 'head'), may hold values from -6 to 6
- block_ids: int32 [64, 16], P('mem'), may hold values from 0 to 511, as said below
- block_counts: int32 [512], replicated, may hold values from 1 to 128
Outputs:
- layer_out: bfloat16 [8192, 4096], P('mem', 'head')
Inputs may be any that keep to these rules, and one draw needn't show every extreme that they name: `block_ids`: row c lists 16 different memory blocks; block b lies on index b // 64 of mem. Over the 8 query blocks of one index of mem, every listed block appears in exactly two rows, at most 16 different listed blocks lie on any one index of mem, and in every draw some index of mem has exactly 16 different blocks listed by every index of mem.
All inputs are finite; a program needn't handle non-finite values.
Results may differ from a plain program's by a relative error of at most 0.015.
The roundings to bfloat16 on the way count: a program that leaves them out, or rounds other values in their place, can miss the bound.
Values may be sent and summed in bfloat16 or wider, within the bound.
A program may use at most 320 MiB of HBM per device.

v0:
```python
import jax
import jax.numpy as jnp
from jax import lax
from jax.sharding import PartitionSpec as P

HD = 128
BLK = 128


def attend(queries, key_rows, value_rows, allowed):
    scores = jnp.einsum(
        "qkgd,skd->kgqs", queries, key_rows, preferred_element_type=jnp.float32
    ) * HD ** (-0.5)
    scores = jnp.where(allowed, scores, -jnp.inf)
    peak_score = jnp.max(scores, axis=-1, keepdims=True)
    weights = jnp.exp(scores - peak_score)
    weights = (weights / jnp.sum(weights, axis=-1, keepdims=True)).astype(jnp.bfloat16)
    return jnp.einsum("kgqs,skd->qkgd", weights, value_rows, preferred_element_type=jnp.float32)


def plan_requests(flat_chosen, blocks_each):
    owner_of = flat_chosen // blocks_each
    local_of = flat_chosen % blocks_each
    order = jnp.arange(flat_chosen.shape[0])
    earlier = order[None, :] < order[:, None]
    first_seen = jnp.ones(flat_chosen.shape, jnp.bool_)
    same_owner = owner_of[:, None] == owner_of[None, :]
    first_rank = jnp.sum((same_owner & earlier & first_seen[None, :]).astype(jnp.int32), axis=1)
    return (owner_of, local_of, first_rank, first_seen)


def on_device(
    tokens, w_query, w_key, w_value, w_out, gate_bias, mem_keys, mem_values, block_ids, block_counts
):
    tok_rows = tokens.shape[0]
    qblk_count = tok_rows // BLK
    topk_count = block_ids.shape[1]
    kv_local = w_key.shape[1] // HD
    heads_local = w_query.shape[1] // HD
    per_kv = heads_local // kv_local
    owners = lax.axis_size("mem")
    blocks_each = mem_keys.shape[0] // BLK
    me_index = lax.axis_index("mem")
    block_cap = max(2, topk_count * qblk_count // owners)
    capacity = 2 * block_cap
    all_chosen = lax.all_gather(block_ids, "mem", axis=0, tiled=True).reshape(
        owners, qblk_count * topk_count
    )

    def send_list(flat_chosen):
        owner_of, local_of, rank_of, first_seen = plan_requests(flat_chosen, blocks_each)
        wanted = (owner_of == me_index) & first_seen
        select = wanted[None, :] & (rank_of[None, :] == jnp.arange(capacity)[:, None])
        return jnp.sum(select.astype(jnp.int32) * local_of[None, :], axis=1)

    send_slots = jax.vmap(send_list)(all_chosen)
    key_blocks = mem_keys.reshape(blocks_each, BLK, kv_local * HD)
    value_blocks = mem_values.reshape(blocks_each, BLK, kv_local * HD)
    send_keys = key_blocks[send_slots]
    send_values = value_blocks[send_slots]
    got_keys, got_values = (
        lax.all_to_all(send_keys, "mem", split_axis=0, concat_axis=0, tiled=True),
        lax.all_to_all(send_values, "mem", split_axis=0, concat_axis=0, tiled=True),
    )
    queries = jnp.dot(tokens, w_query, preferred_element_type=jnp.float32).astype(jnp.bfloat16)
    local_keys = jnp.dot(tokens, w_key, preferred_element_type=jnp.float32).astype(jnp.bfloat16)
    local_values = jnp.dot(tokens, w_value, preferred_element_type=jnp.float32).astype(jnp.bfloat16)
    causal = jnp.arange(tok_rows)[None, :] <= jnp.arange(tok_rows)[:, None]
    local_out = attend(
        queries.reshape(tok_rows, kv_local, per_kv, HD),
        local_keys.reshape(tok_rows, kv_local, HD),
        local_values.reshape(tok_rows, kv_local, HD),
        causal[None, None],
    )
    own_flat = block_ids.reshape(-1)
    owner_of, local_of, rank_of, first_seen = plan_requests(own_flat, blocks_each)
    slot_of = owner_of * capacity + rank_of
    key_rows = got_keys.reshape(owners * capacity, BLK, kv_local * HD)[slot_of]
    value_rows = got_values.reshape(owners * capacity, BLK, kv_local * HD)[slot_of]
    key_rows = key_rows.reshape(qblk_count, topk_count * BLK, kv_local, HD)
    value_rows = value_rows.reshape(qblk_count, topk_count * BLK, kv_local, HD)
    total_blocks = block_counts.shape[0]
    filled = jnp.sum(
        jnp.where(own_flat[:, None] == jnp.arange(total_blocks)[None, :], block_counts[None, :], 0),
        axis=1,
    )
    allowed_mem = (jnp.arange(BLK)[None, :] < filled[:, None]).reshape(qblk_count, topk_count * BLK)

    def memory_block(inputs):
        q_blk, k_blk, v_blk, allow_blk = inputs
        return attend(q_blk, k_blk, v_blk, allow_blk[None, None, None, :])

    mem_out = lax.map(
        memory_block,
        (queries.reshape(qblk_count, BLK, kv_local, per_kv, HD), key_rows, value_rows, allowed_mem),
    )
    mem_out = mem_out.reshape(tok_rows, kv_local, per_kv, HD)
    gate = jax.nn.sigmoid(gate_bias).reshape(kv_local, per_kv)[None, :, :, None]
    attn = (
        (gate * mem_out + (1.0 - gate) * local_out)
        .astype(jnp.bfloat16)
        .reshape(tok_rows, heads_local * HD)
    )
    terms = jnp.dot(attn, w_out, preferred_element_type=jnp.float32)
    return lax.psum_scatter(terms.astype(jnp.bfloat16), "head", scatter_dimension=1, tiled=True)


def solution(mesh):
    in_specs = (
        P("mem", None),
        P(None, "head"),
        P(None, "head"),
        P(None, "head"),
        P("head", None),
        P("head"),
        P("mem", "head"),
        P("mem", "head"),
        P("mem", None),
        P(),
    )
    out_specs = P("mem", "head")
    return jax.shard_map(
        on_device, mesh=mesh, in_specs=in_specs, out_specs=out_specs, check_vma=False
    )
```

profile of v0, /device:TPU:0, one launch (start us, length us, event | category | flops | bytes accessed | tf_op | source)
XLA Modules:
  0.0 1164.7 jit_solution(14783743435537035418)
XLA Ops:
  6.6 32.5 %all_gather.3 = s32[64,16]{1,0:T(8,128)S(1)} all-gather(s32[8,16]{1,0:T(8,128)} %param.20), channel_id=1, replica_groups=mesh['mem'=8,'head'=4] {'mem'}, dimensions={0}, use_global_device_ids=true | all-gather | bytes 4608 | tf_op jit(solution)/shard_map/all_gather | solution.py:46
  39.8 11.5 gather_fusion
  51.3 5.7 all-to-all-start
  57.0 11.6 gather_fusion.2
  68.6 345.2 %all-to-all-done = bf16[8,32,128,256]{3,2,1,0:T(8,128)(2,1)} async-done(((bf16[8,32,128,256]{3,2,1,0:T(8,128)(2,1)}), bf16[8,32,128,256]{3,2,1,0:T(8,128)(2,1)}, u32[]{:S(2)}, u32[]{:S(2)}) %all-to-all-start) | async-done | bytes 16777248 | tf_op jit(solution)/shard_map/all_to_all | solution.py:63
  413.8 5.9 all-to-all-start.1
  420.1 13.8 %convolution_convert_fusion.1 = bf16[1024,1024]{0,1:T(8,128)(2,1)S(1)} fusion(bf16[1024,4096]{1,0:T(8,128)(2,1)} %param.12, bf16[4096,1024]{1,0:T(8,128)(2,1)} %param.13), kind=kOutput, calls=%fused_computation.40 | convolution fusion | flops 8590983168 | bytes 18874368 | tf_op jit(solution)/shard_map/dot_general | solution.py:65
  437.2 4.3 copy.44
  443.2 6.7 convolution_convert_fusion.2
  449.9 6.7 convolution_convert_fusion.3
  456.7 19.2 %fusion.32 = (f32[2,4,1024]{2,1,0:T(4,128)S(1)}, f32[2,4,1024,1024]{2,3,1,0:T(8,128)}) fusion(pred[1024,1024]{0,1:T(8,128)(4,1)S(1)} %iota_compare_fusion, bf16[1024,2,128,1]{0,2,3,1:T(8,128)(2,1)} %bitcast.120, bf16[1024,2,4,128]{0,3,2,1:T(8,128)(2,1)S(1)} %bitcast.117), kind=kOutput, calls=%fused_computation.81 | convolution fusion | flops 2181039104 | bytes 37257216 | tf_op jit(solution)/shard_map/sub | solution.py:16
  475.9 12.3 %gather_fusion.1 = bf16[128,128,256]{2,1,0:T(8,128)(2,1)} fusion(bf16[256,128,256]{2,1,0:T(8,128)(2,1)} %bitcast.13, s32[1024]{0:T(1024)S(1)} %pad_clamp_fusion), kind=kCustom, calls=%fused_computation.1 | custom fusion | bytes 16777728 | tf_op jit(solution)/shard_map/gather | solution.py:79
  488.2 12.5 %reshape.370 = bf16[8,2048,2,128]{3,2,1,0:T(2,128)(2,1)} reshape(bf16[128,128,256]{2,1,0:T(8,128)(2,1)} %gather_fusion.1) | data formatting | bytes 16777216 | tf_op jit(solution)/shard_map/reshape | solution.py:81
  500.7 279.9 %all-to-all-done.1 = bf16[8,32,128,256]{3,2,1,0:T(8,128)(2,1)} async-done(((bf16[8,32,128,256]{3,2,1,0:T(8,128)(2,1)}), bf16[8,32,128,256]{3,2,1,0:T(8,128)(2,1)}, u32[]{:S(2)}, u32[]{:S(2)}) %all-to-all-start.1) | async-done | bytes 16777248 | tf_op jit(solution)/shard_map/all_to_all | solution.py:62
  780.6 12.3 %gather_fusion.3 = bf16[128,128,256]{2,1,0:T(8,128)(2,1)} fusion(bf16[256,128,256]{2,1,0:T(8,128)(2,1)} %bitcast.20, s32[1024]{0:T(1024)S(1)} %pad_clamp_fusion), kind=kCustom, calls=%fused_computation.3 | custom fusion | bytes 16777728 | tf_op jit(solution)/shard_map/gather | solution.py:78
  793.0 12.5 %reshape.371 = bf16[8,2048,2,128]{3,2,1,0:T(2,128)(2,1)} reshape(bf16[128,128,256]{2,1,0:T(8,128)(2,1)} %gather_fusion.3) | data formatting | bytes 16777216 | tf_op jit(solution)/shard_map/reshape | solution.py:80
  805.5 246.9 %while.10 = (s32[]{:T(128)}, f32[8,128,2,4,128]{1,0,4,3,2:T(8,128)}, bf16[8,2048,2,128]{3,2,1,0:T(2,128)(2,1)}, pred[8,2048]{1,0:T(8,128)(4,1)S(1)}, bf16[8,2048...) while((s32[]{:T(128)}, f32[8,128,2,4,128]{1,0,4,3,2:T(8,128)}, ...), condition=%wide.region_7.8_spmd, body=%wide.region_4.7_spmd.sunk | while | flops 1090521088 | bytes 43792992 | solution.py:93
  805.6 2.7 constant_dynamic-slice_fusion.3
  810.6 5.9 fusion.54
  817.3 4.1 fusion.55
  821.4 15.1 %dynamic_update_slice.5 = f32[8,128,2,4,128]{1,0,4,3,2:T(8,128)} dynamic-update-slice(f32[8,128,2,4,128]{1,0,4,3,2:T(8,128)} %get-tuple-element.136, f32[1,128,2,4,128]{1,0,4,3,2:T(1,128)S(1)} %bitcast.114, s32[]{:T(128)} %get-tuple-element.135, s32[]{:T(128)} %constant.69.clone.1..sunk, s32[]{:T(128)} %constant.69.clone.1..sunk, s32[]{:T(128)} %constant.69.clone.1..sunk, s32[]{:T(128)} %constant.69.clone.1..sunk) | dynamic-update-slice | bytes 1048580 | tf_op jit(solution)/shard_map/while/body/jit(dynamic_update_index_in_dim)/dynamic_update_slice | solution.py:93
  836.5 2.7 constant_dynamic-slice_fusion.3
  841.4 5.9 fusion.54
  848.1 4.1 fusion.55
  852.2 15.1 %dynamic_update_slice.5 = f32[8,128,2,4,128]{1,0,4,3,2:T(8,128)} dynamic-update-slice(f32[8,128,2,4,128]{1,0,4,3,2:T(8,128)} %get-tuple-element.136, f32[1,128,2,4,128]{1,0,4,3,2:T(1,128)S(1)} %bitcast.114, s32[]{:T(128)} %get-tuple-element.135, s32[]{:T(128)} %constant.69.clone.1..sunk, s32[]{:T(128)} %constant.69.clone.1..sunk, s32[]{:T(128)} %constant.69.clone.1..sunk, s32[]{:T(128)} %constant.69.clone.1..sunk) | dynamic-update-slice | bytes 1048580 | tf_op jit(solution)/shard_map/while/body/jit(dynamic_update_index_in_dim)/dynamic_update_slice | solution.py:93
  872.3 5.9 fusion.54
  879.0 4.1 fusion.55
  883.1 15.1 %dynamic_update_slice.5 = f32[8,128,2,4,128]{1,0,4,3,2:T(8,128)} dynamic-update-slice(f32[8,128,2,4,128]{1,0,4,3,2:T(8,128)} %get-tuple-element.136, f32[1,128,2,4,128]{1,0,4,3,2:T(1,128)S(1)} %bitcast.114, s32[]{:T(128)} %get-tuple-element.135, s32[]{:T(128)} %constant.69.clone.1..sunk, s32[]{:T(128)} %constant.69.clone.1..sunk, s32[]{:T(128)} %constant.69.clone.1..sunk, s32[]{:T(128)} %constant.69.clone.1..sunk) | dynamic-update-slice | bytes 1048580 | tf_op jit(solution)/shard_map/while/body/jit(dynamic_update_index_in_dim)/dynamic_update_slice | solution.py:93
  903.1 5.9 fusion.54
  909.8 4.1 fusion.55
  913.9 15.1 %dynamic_update_slice.5 = f32[8,128,2,4,128]{1,0,4,3,2:T(8,128)} dynamic-update-slice(f32[8,128,2,4,128]{1,0,4,3,2:T(8,128)} %get-tuple-element.136, f32[1,128,2,4,128]{1,0,4,3,2:T(1,128)S(1)} %bitcast.114, s32[]{:T(128)} %get-tuple-element.135, s32[]{:T(128)} %constant.69.clone.1..sunk, s32[]{:T(128)} %constant.69.clone.1..sunk, s32[]{:T(128)} %constant.69.clone.1..sunk, s32[]{:T(128)} %constant.69.clone.1..sunk) | dynamic-update-slice | bytes 1048580 | tf_op jit(solution)/shard_map/while/body/jit(dynamic_update_index_in_dim)/dynamic_update_slice | solution.py:93
  929.0 2.7 constant_dynamic-slice_fusion.3
  934.0 5.9 fusion.54
  940.7 4.1 fusion.55
  944.8 15.1 %dynamic_update_slice.5 = f32[8,128,2,4,128]{1,0,4,3,2:T(8,128)} dynamic-update-slice(f32[8,128,2,4,128]{1,0,4,3,2:T(8,128)} %get-tuple-element.136, f32[1,128,2,4,128]{1,0,4,3,2:T(1,128)S(1)} %bitcast.114, s32[]{:T(128)} %get-tuple-element.135, s32[]{:T(128)} %constant.69.clone.1..sunk, s32[]{:T(128)} %constant.69.clone.1..sunk, s32[]{:T(128)} %constant.69.clone.1..sunk, s32[]{:T(128)} %constant.69.clone.1..sunk) | dynamic-update-slice | bytes 1048580 | tf_op jit(solution)/shard_map/while/body/jit(dynamic_update_index_in_dim)/dynamic_update_slice | solution.py:93
  964.8 5.9 fusion.54
  971.5 4.1 fusion.55
  975.6 15.1 %dynamic_update_slice.5 = f32[8,128,2,4,128]{1,0,4,3,2:T(8,128)} dynamic-update-slice(f32[8,128,2,4,128]{1,0,4,3,2:T(8,128)} %get-tuple-element.136, f32[1,128,2,4,128]{1,0,4,3,2:T(1,128)S(1)} %bitcast.114, s32[]{:T(128)} %get-tuple-element.135, s32[]{:T(128)} %constant.69.clone.1..sunk, s32[]{:T(128)} %constant.69.clone.1..sunk, s32[]{:T(128)} %constant.69.clone.1..sunk, s32[]{:T(128)} %constant.69.clone.1..sunk) | dynamic-update-slice | bytes 1048580 | tf_op jit(solution)/shard_map/while/body/jit(dynamic_update_index_in_dim)/dynamic_update_slice | solution.py:93
  995.7 5.9 fusion.54
  1002.3 4.1 fusion.55
  1006.5 15.1 %dynamic_update_slice.5 = f32[8,128,2,4,128]{1,0,4,3,2:T(8,128)} dynamic-update-slice(f32[8,128,2,4,128]{1,0,4,3,2:T(8,128)} %get-tuple-element.136, f32[1,128,2,4,128]{1,0,4,3,2:T(1,128)S(1)} %bitcast.114, s32[]{:T(128)} %get-tuple-element.135, s32[]{:T(128)} %constant.69.clone.1..sunk, s32[]{:T(128)} %constant.69.clone.1..sunk, s32[]{:T(128)} %constant.69.clone.1..sunk, s32[]{:T(128)} %constant.69.clone.1..sunk) | dynamic-update-slice | bytes 1048580 | tf_op jit(solution)/shard_map/while/body/jit(dynamic_update_index_in_dim)/dynamic_update_slice | solution.py:93
  1026.5 5.9 fusion.54
  1033.2 4.1 fusion.55
  1037.3 15.1 %dynamic_update_slice.5 = f32[8,128,2,4,128]{1,0,4,3,2:T(8,128)} dynamic-update-slice(f32[8,128,2,4,128]{1,0,4,3,2:T(8,128)} %get-tuple-element.136, f32[1,128,2,4,128]{1,0,4,3,2:T(1,128)S(1)} %bitcast.114, s32[]{:T(128)} %get-tuple-element.135, s32[]{:T(128)} %constant.69.clone.1..sunk, s32[]{:T(128)} %constant.69.clone.1..sunk, s32[]{:T(128)} %constant.69.clone.1..sunk, s32[]{:T(128)} %constant.69.clone.1..sunk) | dynamic-update-slice | bytes 1048580 | tf_op jit(solution)/shard_map/while/body/jit(dynamic_update_index_in_dim)/dynamic_update_slice | solution.py:93
  1052.4 5.0 reshape.327
  1057.4 13.3 %fusion.22 = bf16[1024,2,4,128]{0,3,2,1:T(8,128)(2,1)S(1)} fusion(f32[1024,2,4,128]{0,3,2,1:T(8,128)} %reshape.327, bf16[1024,2,128,1]{0,2,3,1:T(8,128)(2,1)S(1)} %bitcast.119, f32[2,4,1024,1024]{2,3,1,0:T(8,128)} %get-tuple-element.81, f32[2,4,1024]{2,1,0:T(4,128)S(1)} %get-tuple-element.80, f32[2,4]{1,0:T(2,128)S(1)} %copy-done.8, f32[2,4]{1,0:T(2,128)S(1)} %copy-done.7), kind=kOutput, calls=%fused_computation.37 | convolution fusion | flops 2168455168 | bytes 40403008 | tf_op jit(solution)/shard_map/kgqs,skd->qkgd/dot_general | solution.py:18
  1070.7 14.9 %convolution_convert_fusion = bf16[1024,4096]{1,0:T(8,128)(2,1)} fusion(bf16[1024,1024]{0,1:T(8,128)(2,1)S(1)} %bitcast.118, bf16[1024,4096]{1,0:T(8,128)(2,1)} %param.16), kind=kOutput, calls=%fused_computation.35 | convolution fusion | flops 8594128896 | bytes 18874368 | tf_op jit(solution)/shard_map/dot_general | solution.py:104
  1085.7 71.9 %reduce-scatter.2.cloned.1.call-done = bf16[1024,1024]{1,0:T(8,128)(2,1)} async-done(((bf16[1024,4096]{1,0:T(8,128)(2,1)}), bf16[1024,1024]{1,0:T(8,128)(2,1)}) %reduce-scatter.2.cloned.1.call-update) | async-done | bytes 2097168 | tf_op jit(solution)/shard_map/reduce_scatter | solution.py:105
  (81 shorter events, 44.0 us)
Async XLA Ops:
  6.5 436.7 %copy-start = (bf16[4096,256]{1,0:T(8,128)(2,1)S(1)}, bf16[4096,256]{1,0:T(8,128)(2,1)}, u32[]{:S(2)}) copy-start(bf16[4096,256]{1,0:T(8,128)(2,1)} %param.14) | copy-start | bytes 6291460
  51.3 362.5 %all-to-all-start = ((bf16[8,32,128,256]{3,2,1,0:T(8,128)(2,1)}), bf16[8,32,128,256]{3,2,1,0:T(8,128)(2,1)}, u32[]{:S(2)}, u32[]{:S(2)}) async-start(bf16[8,32,128,256]{3,2,1,0:T(8,128)(2,1)} %bitcast.111), calls=%async_computation | async-start | bytes 33554432 | tf_op jit(solution)/shard_map/all_to_all | solution.py:63
  413.8 6.2 copy-start.4
  413.8 366.9 %all-to-all-start.1 = ((bf16[8,32,128,256]{3,2,1,0:T(8,128)(2,1)}), bf16[8,32,128,256]{3,2,1,0:T(8,128)(2,1)}, u32[]{:S(2)}, u32[]{:S(2)}) async-start(bf16[8,32,128,256]{3,2,1,0:T(8,128)(2,1)} %bitcast.110), calls=%async_computation.1 | async-start | bytes 33554432 | tf_op jit(solution)/shard_map/all_to_all | solution.py:62
  419.6 738.0 %reduce-scatter.2.cloned.1.call-start = ((), (), s32[]{:S(2)}) async-start(), calls=%async_computation.3 | async-start | bytes 10485760 | tf_op jit(solution)/shard_map/reduce_scatter | solution.py:105
  433.9 1.3 copy-start.2
  433.9 7.6 copy-start.5
  433.9 7.9 copy-start.10
  441.9 0.6 copy-start.6
  443.2 6.7 copy-start.9
  449.9 6.7 copy-start.3
  1052.4 5.0 copy-start.7
  1052.4 5.0 copy-start.8
  1052.4 5.0 copy-start.11
  1070.7 86.9 %copy-start.1 = (bf16[4096,256]{1,0:T(8,128)(2,1)S(1)}, bf16[4096,256]{1,0:T(8,128)(2,1)}, u32[]{:S(2)}) copy-start(bf16[4096,256]{1,0:T(8,128)(2,1)} %param.14) | copy-start | bytes 6291460
Sparse Core Ops, SparseCore 0:
  1085.8 71.7 reduce-scatter.1
where the time goes:
time: 1170 us; the launch traced here: 1160 us
  waiting for transfers between devices  697 us (60%)
  local copies, waits for them, and re-layouts  235 us (20%)
  matrix products  125 us (11%)
  other arithmetic  48.9 us (4%)
  blocking collectives  32.5 us (3%)
  between operations  13.8 us (1%)
  starting transfers between devices  11.9 us (1%)
    all_to_all x1, waiting for transfers between devices, on_device(): lax.all_to_all(send_values, 'mem', split_axis=0, concat_axis=0, tiled=True)  345 us
    all_to_all x1, waiting for transfers between devices, on_device(): lax.all_to_all(send_keys, 'mem', split_axis=0, concat_axis=0, tiled=True)  280 us
    dynamic_update_slice x8, local copies, waits for them, and re-layouts, on_device(): lax.map(memory_block, (queries.reshape(qblk_count, BLK, kv_local, per_kv,...  121 us
    reduce_scatter x1, waiting for transfers between devices, on_device(): lax.psum_scatter(terms.astype(jnp.bfloat16), 'head', scatter_dimension=1,...  71.9 us
    sub x8, other arithmetic, attend(): weights = jnp.exp(scores - peak_score)  46.9 us
    dot_general x9, matrix products, attend(): jnp.einsum('kgqs,skd->qkgd', weights, value_rows, preferred_element_type=...  46.1 us
    all_gather x1, blocking collectives, on_device(): lax.all_gather(block_ids, 'mem', axis=0, tiled=True)  32.5 us
    dynamic_slice x24, local copies, waits for them, and re-layouts, on_device(): lax.map(memory_block, (queries.reshape(qblk_count, BLK, kv_local, per_kv,...  28.1 us
  transfers between devices with their start and end apart: 3, of which 3 were waited for; matrix products, arithmetic and copies ran while one was open for 8% of the time, Pallas kernels for 0%

commit v1 on v0

--- a/solution.py
+++ b/solution.py
@@ -5,6 +5,22 @@
 
 HD = 128
 BLK = 128
+
+
+def swapped_with_each(x, axis, split, join):
+    ways, here = (lax.axis_size(axis), lax.axis_index(axis))
+    width = x.shape[split] // ways
+    shape = list(x.shape)
+    shape[split] = width
+    height = shape[join]
+    shape[join] = height * ways
+    full = jnp.zeros(shape, x.dtype)
+    for mask in range(ways):
+        part = lax.dynamic_slice_in_dim(x, (here ^ mask) * width, width, axis=split)
+        if mask:
+            part = lax.ppermute(part, axis, [(d, d ^ mask) for d in range(ways)])
+        full = lax.dynamic_update_slice_in_dim(full, part, (here ^ mask) * height, axis=join)
+    return full
 
 
 def attend(queries, key_rows, value_rows, allowed):
@@ -60,7 +76,7 @@
     send_values = value_blocks[send_slots]
     got_keys, got_values = (
         lax.all_to_all(send_keys, "mem", split_axis=0, concat_axis=0, tiled=True),
-        lax.all_to_all(send_values, "mem", split_axis=0, concat_axis=0, tiled=True),
+        swapped_with_each(send_values, "mem", 0, 0),
     )
     queries = jnp.dot(tokens, w_query, preferred_element_type=jnp.float32).astype(jnp.bfloat16)
     local_keys = jnp.dot(tokens, w_key, preferred_element_type=jnp.float32).astype(jnp.bfloat16)

time: 1170 us -> 1190 us (1.017)
  local copies, waits for them, and re-layouts: 235 us -> 270 us
  waiting for transfers between devices: 697 us -> 670 us
  starting transfers between devices: 11.9 us -> 26.2 us
    ppermute x0 -> x7, waiting for transfers between devices: none -> 518 us  [swapped_with_each(): part = lax.ppermute(part, axis, [(d, d ^ mask) for d in range(ways)])]
    all_to_all x1 -> x0, waiting for transfers between devices: 345 us -> none  [on_device(): lax.all_to_all(send_values, 'mem', split_axis=0, concat_axis=0, tiled=True)]
    all_to_all x1, waiting for transfers between devices: 280 us -> 0.01 us  [on_device(): lax.all_to_all(send_keys, 'mem', split_axis=0, concat_axis=0, tiled=True)]
    reduce_scatter x1, waiting for transfers between devices: 71.9 us -> 152 us  [on_device(): lax.psum_scatter(terms.astype(jnp.bfloat16), 'head', scatter_dimension=1,...]
    dynamic_update_slice x0 -> x7, local copies, waits for them, and re-layouts: none -> 20.5 us  [swapped_with_each(): lax.dynamic_update_slice_in_dim(full, part, (here ^ mask) * height, axis=...]
    ppermute x0 -> x7, starting transfers between devices: none -> 20.2 us  [swapped_with_each(): part = lax.ppermute(part, axis, [(d, d ^ mask) for d in range(ways)])]
  transfers between devices with their start and end apart: 3 -> 9, of which waited for: 3 -> 6; matrix products, arithmetic and copies ran while one was open for 8% -> 10% of each run, Pallas kernels for 0% -> 0%
where the time goes in v1:
time: 1190 us
  waiting for transfers between devices  670 us (56%)
  local copies, waits for them, and re-layouts  270 us (23%)
  matrix products  125 us (11%)
  other arithmetic  48.9 us (4%)
  blocking collectives  32.5 us (3%)
  starting transfers between devices  26.2 us (2%)
  between operations  13.8 us (1%)
    ppermute x7, waiting for transfers between devices, swapped_with_each(): part = lax.ppermute(part, axis, [(d, d ^ mask) for d in range(ways)])  518 us
    reduce_scatter x1, waiting for transfers between devices, on_device(): lax.psum_scatter(terms.astype(jnp.bfloat16), 'head', scatter_dimension=1,...  152 us
    dynamic_update_slice x8, local copies, waits for them, and re-layouts, on_device(): lax.map(memory_block, (queries.reshape(qblk_count, BLK, kv_local, per_kv,...  121 us
    sub x8, other arithmetic, attend(): weights = jnp.exp(scores - peak_score)  46.9 us
    dot_general x9, matrix products, attend(): jnp.einsum('kgqs,skd->qkgd', weights, value_rows, preferred_element_type=...  46.1 us
    all_gather x1, blocking collectives, on_device(): lax.all_gather(block_ids, 'mem', axis=0, tiled=True)  32.5 us
    dynamic_slice x24, local copies, waits for them, and re-layouts, on_device(): lax.map(memory_block, (queries.reshape(qblk_count, BLK, kv_local, per_kv,...  28.1 us
  transfers between devices with their start and end apart: 9, of which 6 were waited for; matrix products, arithmetic and copies ran while one was open for 10% of the time, Pallas kernels for 0%

profile of v1, /device:TPU:0, one launch (start us, length us, event | category | flops | bytes accessed | tf_op | source)
XLA Modules:
  0.0 1186.6 jit_solution(16049246838863786012)
XLA Ops:
  6.6 32.5 %all_gather.3 = s32[64,16]{1,0:T(8,128)S(1)} all-gather(s32[8,16]{1,0:T(8,128)} %param.20), channel_id=1, replica_groups=mesh['mem'=8,'head'=4] {'mem'}, dimensions={0}, use_global_device_ids=true | all-gather | bytes 4608 | tf_op jit(solution)/shard_map/all_gather | solution.py:62
  39.8 11.6 gather_fusion.2
  51.4 5.7 all-to-all-start
  57.5 11.5 gather_fusion
  68.9 8.4 broadcast_in_dim.42
  80.4 6.0 constant_dynamic-slice_fusion.2
  95.5 6.6 convolution_convert_fusion.2
  102.1 13.8 %convolution_convert_fusion.1 = bf16[1024,1024]{0,1:T(8,128)(2,1)S(1)} fusion(bf16[1024,4096]{1,0:T(8,128)(2,1)} %param.12, bf16[4096,1024]{1,0:T(8,128)(2,1)} %param.13), kind=kOutput, calls=%fused_computation.41 | convolution fusion | flops 8590983168 | bytes 18874368 | tf_op jit(solution)/shard_map/dot_general | solution.py:81
  115.8 19.4 %fusion.32 = (f32[2,4,1024]{2,1,0:T(4,128)S(1)}, f32[2,4,1024,1024]{2,3,1,0:T(8,128)}) fusion(pred[1024,1024]{0,1:T(8,128)(4,1)S(1)} %iota_compare_fusion, bf16[1024,2,128,1]{0,2,3,1:T(8,128)(2,1)} %bitcast.121, bf16[1024,2,4,128]{0,3,2,1:T(8,128)(2,1)S(1)} %bitcast.117), kind=kOutput, calls=%fused_computation.96 | convolution fusion | flops 2181039104 | bytes 37257216 | tf_op jit(solution)/shard_map/sub | solution.py:32
  135.4 99.9 %collective-permute-done = bf16[1,32,128,256]{3,2,1,0:T(8,128)(2,1)} collective-permute-done((bf16[1,32,128,256]{3,2,1,0:T(8,128)(2,1)}, bf16[1,32,128,256]{3,2,1,0:T(8,128)(2,1)}, u32[]{:S(2)}, u32[]{:S(2)}) %collective-permute-start) | collective-permute-done | bytes 2097184 | tf_op jit(solution)/shard_map/ppermute | solution.py:21
  235.3 8.3 collective-permute-start.5
  248.7 125.1 %collective-permute-done.1 = bf16[1,32,128,256]{3,2,1,0:T(8,128)(2,1)} collective-permute-done((bf16[1,32,128,256]{3,2,1,0:T(8,128)(2,1)}, bf16[1,32,128,256]{3,2,1,0:T(8,128)(2,1)}, u32[]{:S(2)}, u32[]{:S(2)}) %collective-permute-start.1) | collective-permute-done | bytes 2097184 | tf_op jit(solution)/shard_map/ppermute | solution.py:21
  373.8 4.1 collective-permute-start.6
  378.0 6.3 convolution_convert_fusion.3
  390.6 28.1 %collective-permute-done.2 = bf16[1,32,128,256]{3,2,1,0:T(8,128)(2,1)} collective-permute-done((bf16[1,32,128,256]{3,2,1,0:T(8,128)(2,1)}, bf16[1,32,128,256]{3,2,1,0:T(8,128)(2,1)}, u32[]{:S(2)}, u32[]{:S(2)}) %collective-permute-start.2) | collective-permute-done | bytes 2097184 | tf_op jit(solution)/shard_map/ppermute | solution.py:21
  421.8 224.3 %collective-permute-done.3 = bf16[1,32,128,256]{3,2,1,0:T(8,128)(2,1)} collective-permute-done((bf16[1,32,128,256]{3,2,1,0:T(8,128)(2,1)}, bf16[1,32,128,256]{3,2,1,0:T(8,128)(2,1)}, u32[]{:S(2)}, u32[]{:S(2)}) %collective-permute-start.3) | collective-permute-done | bytes 2097184 | tf_op jit(solution)/shard_map/ppermute | solution.py:21
  649.2 41.0 %collective-permute-done.4 = bf16[1,32,128,256]{3,2,1,0:T(8,128)(2,1)} collective-permute-done((bf16[1,32,128,256]{3,2,1,0:T(8,128)(2,1)}, bf16[1,32,128,256]{3,2,1,0:T(8,128)(2,1)}, u32[]{:S(2)}, u32[]{:S(2)}) %collective-permute-start.4) | collective-permute-done | bytes 2097184 | tf_op jit(solution)/shard_map/ppermute | solution.py:21
  698.1 12.3 %gather_fusion.1 = bf16[128,128,256]{2,1,0:T(8,128)(2,1)} fusion(bf16[256,128,256]{2,1,0:T(8,128)(2,1)} %bitcast.114, s32[1024]{0:T(1024)S(1)} %pad_clamp_fusion), kind=kCustom, calls=%fused_computation.1 | custom fusion | bytes 16777728 | tf_op jit(solution)/shard_map/gather | solution.py:95
  710.4 12.5 %reshape.370 = bf16[8,2048,2,128]{3,2,1,0:T(2,128)(2,1)} reshape(bf16[128,128,256]{2,1,0:T(8,128)(2,1)} %gather_fusion.1) | data formatting | bytes 16777216 | tf_op jit(solution)/shard_map/reshape | solution.py:97
  723.0 12.5 %gather_fusion.3 = bf16[128,128,256]{2,1,0:T(8,128)(2,1)} fusion(bf16[256,128,256]{2,1,0:T(8,128)(2,1)} %bitcast.20, s32[1024]{0:T(1024)S(1)} %pad_clamp_fusion), kind=kCustom, calls=%fused_computation.3 | custom fusion | bytes 16777728 | tf_op jit(solution)/shard_map/gather | solution.py:94
  735.5 12.5 %reshape.371 = bf16[8,2048,2,128]{3,2,1,0:T(2,128)(2,1)} reshape(bf16[128,128,256]{2,1,0:T(8,128)(2,1)} %gather_fusion.3) | data formatting | bytes 16777216 | tf_op jit(solution)/shard_map/reshape | solution.py:96
  748.0 246.8 %while.10 = (s32[]{:T(128)}, f32[8,128,2,4,128]{1,0,4,3,2:T(8,128)}, bf16[8,2048,2,128]{3,2,1,0:T(2,128)(2,1)}, pred[8,2048]{1,0:T(8,128)(4,1)S(1)}, bf16[8,2048...) while((s32[]{:T(128)}, f32[8,128,2,4,128]{1,0,4,3,2:T(8,128)}, ...), condition=%wide.region_7.8_spmd, body=%wide.region_4.7_spmd.sunk | while | flops 1090521088 | bytes 43792992 | solution.py:109
  752.9 5.9 fusion.54
  759.6 4.1 fusion.55
  763.7 15.1 %dynamic_update_slice.45 = f32[8,128,2,4,128]{1,0,4,3,2:T(8,128)} dynamic-update-slice(f32[8,128,2,4,128]{1,0,4,3,2:T(8,128)} %get-tuple-element.144, f32[1,128,2,4,128]{1,0,4,3,2:T(1,128)S(1)} %bitcast.115, s32[]{:T(128)} %get-tuple-element.143, s32[]{:T(128)} %constant.48.clone.1..sunk, s32[]{:T(128)} %constant.48.clone.1..sunk, s32[]{:T(128)} %constant.48.clone.1..sunk, s32[]{:T(128)} %constant.48.clone.1..sunk) | dynamic-update-slice | bytes 1048580 | tf_op jit(solution)/shard_map/while/body/jit(dynamic_update_index_in_dim)/dynamic_update_slice | solution.py:109
  783.8 5.9 fusion.54
  790.5 4.1 fusion.55
  794.6 15.1 %dynamic_update_slice.45 = f32[8,128,2,4,128]{1,0,4,3,2:T(8,128)} dynamic-update-slice(f32[8,128,2,4,128]{1,0,4,3,2:T(8,128)} %get-tuple-element.144, f32[1,128,2,4,128]{1,0,4,3,2:T(1,128)S(1)} %bitcast.115, s32[]{:T(128)} %get-tuple-element.143, s32[]{:T(128)} %constant.48.clone.1..sunk, s32[]{:T(128)} %constant.48.clone.1..sunk, s32[]{:T(128)} %constant.48.clone.1..sunk, s32[]{:T(128)} %constant.48.clone.1..sunk) | dynamic-update-slice | bytes 1048580 | tf_op jit(solution)/shard_map/while/body/jit(dynamic_update_index_in_dim)/dynamic_update_slice | solution.py:109
  814.6 5.9 fusion.54
  821.3 4.1 fusion.55
  825.4 15.1 %dynamic_update_slice.45 = f32[8,128,2,4,128]{1,0,4,3,2:T(8,128)} dynamic-update-slice(f32[8,128,2,4,128]{1,0,4,3,2:T(8,128)} %get-tuple-element.144, f32[1,128,2,4,128]{1,0,4,3,2:T(1,128)S(1)} %bitcast.115, s32[]{:T(128)} %get-tuple-element.143, s32[]{:T(128)} %constant.48.clone.1..sunk, s32[]{:T(128)} %constant.48.clone.1..sunk, s32[]{:T(128)} %constant.48.clone.1..sunk, s32[]{:T(128)} %constant.48.clone.1..sunk) | dynamic-update-slice | bytes 1048580 | tf_op jit(solution)/shard_map/while/body/jit(dynamic_update_index_in_dim)/dynamic_update_slice | solution.py:109
  845.5 5.9 fusion.54
  852.2 4.1 fusion.55
  856.3 15.1 %dynamic_update_slice.45 = f32[8,128,2,4,128]{1,0,4,3,2:T(8,128)} dynamic-update-slice(f32[8,128,2,4,128]{1,0,4,3,2:T(8,128)} %get-tuple-element.144, f32[1,128,2,4,128]{1,0,4,3,2:T(1,128)S(1)} %bitcast.115, s32[]{:T(128)} %get-tuple-element.143, s32[]{:T(128)} %constant.48.clone.1..sunk, s32[]{:T(128)} %constant.48.clone.1..sunk, s32[]{:T(128)} %constant.48.clone.1..sunk, s32[]{:T(128)} %constant.48.clone.1..sunk) | dynamic-update-slice | bytes 1048580 | tf_op jit(solution)/shard_map/while/body/jit(dynamic_update_index_in_dim)/dynamic_update_slice | solution.py:109
  876.3 5.9 fusion.54
  883.0 4.1 fusion.55
  887.1 15.1 %dynamic_update_slice.45 = f32[8,128,2,4,128]{1,0,4,3,2:T(8,128)} dynamic-update-slice(f32[8,128,2,4,128]{1,0,4,3,2:T(8,128)} %get-tuple-element.144, f32[1,128,2,4,128]{1,0,4,3,2:T(1,128)S(1)} %bitcast.115, s32[]{:T(128)} %get-tuple-element.143, s32[]{:T(128)} %constant.48.clone.1..sunk, s32[]{:T(128)} %constant.48.clone.1..sunk, s32[]{:T(128)} %constant.48.clone.1..sunk, s32[]{:T(128)} %constant.48.clone.1..sunk) | dynamic-update-slice | bytes 1048580 | tf_op jit(solution)/shard_map/while/body/jit(dynamic_update_index_in_dim)/dynamic_update_slice | solution.py:109
  907.2 5.9 fusion.54
  913.8 4.1 fusion.55
  918.0 15.1 %dynamic_update_slice.45 = f32[8,128,2,4,128]{1,0,4,3,2:T(8,128)} dynamic-update-slice(f32[8,128,2,4,128]{1,0,4,3,2:T(8,128)} %get-tuple-element.144, f32[1,128,2,4,128]{1,0,4,3,2:T(1,128)S(1)} %bitcast.115, s32[]{:T(128)} %get-tuple-element.143, s32[]{:T(128)} %constant.48.clone.1..sunk, s32[]{:T(128)} %constant.48.clone.1..sunk, s32[]{:T(128)} %constant.48.clone.1..sunk, s32[]{:T(128)} %constant.48.clone.1..sunk) | dynamic-update-slice | bytes 1048580 | tf_op jit(solution)/shard_map/while/body/jit(dynamic_update_index_in_dim)/dynamic_update_slice | solution.py:109
  938.0 5.9 fusion.54
  948.8 15.1 %dynamic_update_slice.45 = f32[8,128,2,4,128]{1,0,4,3,2:T(8,128)} dynamic-update-slice(f32[8,128,2,4,128]{1,0,4,3,2:T(8,128)} %get-tuple-element.144, f32[1,128,2,4,128]{1,0,4,3,2:T(1,128)S(1)} %bitcast.115, s32[]{:T(128)} %get-tuple-element.143, s32[]{:T(128)} %constant.48.clone.1..sunk, s32[]{:T(128)} %constant.48.clone.1..sunk, s32[]{:T(128)} %constant.48.clone.1..sunk, s32[]{:T(128)} %constant.48.clone.1..sunk) | dynamic-update-slice | bytes 1048580 | tf_op jit(solution)/shard_map/while/body/jit(dynamic_update_index_in_dim)/dynamic_update_slice | solution.py:109
  968.9 5.9 fusion.54
  979.6 15.1 %dynamic_update_slice.45 = f32[8,128,2,4,128]{1,0,4,3,2:T(8,128)} dynamic-update-slice(f32[8,128,2,4,128]{1,0,4,3,2:T(8,128)} %get-tuple-element.144, f32[1,128,2,4,128]{1,0,4,3,2:T(1,128)S(1)} %bitcast.115, s32[]{:T(128)} %get-tuple-element.143, s32[]{:T(128)} %constant.48.clone.1..sunk, s32[]{:T(128)} %constant.48.clone.1..sunk, s32[]{:T(128)} %constant.48.clone.1..sunk, s32[]{:T(128)} %constant.48.clone.1..sunk) | dynamic-update-slice | bytes 1048580 | tf_op jit(solution)/shard_map/while/body/jit(dynamic_update_index_in_dim)/dynamic_update_slice | solution.py:109
  994.8 4.9 reshape.327
  999.7 13.3 %fusion.22 = bf16[1024,2,4,128]{0,3,2,1:T(8,128)(2,1)S(1)} fusion(f32[1024,2,4,128]{0,3,2,1:T(8,128)} %reshape.327, bf16[1024,2,128,1]{0,2,3,1:T(8,128)(2,1)S(1)} %bitcast.120, f32[2,4,1024,1024]{2,3,1,0:T(8,128)} %get-tuple-element.89, f32[2,4,1024]{2,1,0:T(4,128)S(1)} %get-tuple-element.88, f32[2,4]{1,0:T(2,128)S(1)} %copy-done.8, f32[2,4]{1,0:T(2,128)S(1)} %copy-done.7), kind=kOutput, calls=%fused_computation.37 | convolution fusion | flops 2168455168 | bytes 40403008 | tf_op jit(solution)/shard_map/kgqs,skd->qkgd/dot_general | solution.py:34
  1013.0 14.9 %convolution_convert_fusion = bf16[1024,4096]{1,0:T(8,128)(2,1)} fusion(bf16[1024,1024]{0,1:T(8,128)(2,1)S(1)} %bitcast.119, bf16[1024,4096]{1,0:T(8,128)(2,1)} %param.16), kind=kOutput, calls=%fused_computation.35 | convolution fusion | flops 8594128896 | bytes 18874368 | tf_op jit(solution)/shard_map/dot_general | solution.py:120
  1028.0 151.6 %reduce-scatter.2.cloned.1.call-done = bf16[1024,1024]{1,0:T(8,128)(2,1)} async-done(((bf16[1024,4096]{1,0:T(8,128)(2,1)}), bf16[1024,1024]{1,0:T(8,128)(2,1)}) %reduce-scatter.2.cloned.1.call-update) | async-done | bytes 2097168 | tf_op jit(solution)/shard_map/reduce_scatter | solution.py:121
  (98 shorter events, 93.0 us)
Async XLA Ops:
  6.5 88.9 %copy-start = (bf16[4096,256]{1,0:T(8,128)(2,1)S(1)}, bf16[4096,256]{1,0:T(8,128)(2,1)}, u32[]{:S(2)}) copy-start(bf16[4096,256]{1,0:T(8,128)(2,1)} %param.14) | copy-start | bytes 6291460
  51.4 671.6 %all-to-all-start = ((bf16[8,32,128,256]{3,2,1,0:T(8,128)(2,1)}), bf16[8,32,128,256]{3,2,1,0:T(8,128)(2,1)}, u32[]{:S(2)}, u32[]{:S(2)}) async-start(bf16[8,32,128,256]{3,2,1,0:T(8,128)(2,1)} %bitcast.110), calls=%async_computation | async-start | bytes 33554432 | tf_op jit(solution)/shard_map/all_to_all | solution.py:78
  57.1 1122.4 %reduce-scatter.2.cloned.1.call-start = ((), (), s32[]{:S(2)}) async-start(), calls=%async_computation.2 | async-start | bytes 10485760 | tf_op jit(solution)/shard_map/reduce_scatter | solution.py:121
  68.9 11.5 copy-start.2
  80.4 13.7 %copy-start.4 = (s32[8,16]{1,0:T(8,128)S(1)}, s32[8,16]{1,0:T(8,128)}, u32[]{:S(2)}) copy-start(s32[8,16]{1,0:T(8,128)} %param.20) | copy-start | bytes 1540
  80.4 13.9 %copy-start.9 = (f32[8]{0:T(128)S(1)}, f32[8]{0:T(128)}, u32[]{:S(2)}) copy-start(f32[8]{0:T(128)} %param.17) | copy-start | bytes 100
  86.4 148.9 %collective-permute-start = (bf16[1,32,128,256]{3,2,1,0:T(8,128)(2,1)}, bf16[1,32,128,256]{3,2,1,0:T(8,128)(2,1)}, u32[]{:S(2)}, u32[]{:S(2)}) collective-permute-start(bf16[1,32,128,256]{3,2,1,0:T(8,128)(2,1)} %get-tuple-element.86), channel_id=1, source_target_pairs={{0,4},{4,0},{8,12},{12,8},{16,20},{20,16},{24,28},{28,24},{1,5},{5... | collective-permute-start | bytes 6291464 | tf_op jit(solution)/shard_map/ppermute | solution.py:21
  88.3 285.5 %collective-permute-start.1 = (bf16[1,32,128,256]{3,2,1,0:T(8,128)(2,1)}, bf16[1,32,128,256]{3,2,1,0:T(8,128)(2,1)}, u32[]{:S(2)}, u32[]{:S(2)}) collective-permute-start(bf16[1,32,128,256]{3,2,1,0:T(8,128)(2,1)} %get-tuple-element.85), channel_id=1, source_target_pairs={{0,8},{4,12},{8,0},{12,4},{16,24},{20,28},{24,16},{28,20},{1,9},{5... | collective-permute-start | bytes 6291464 | tf_op jit(solution)/shard_map/ppermute | solution.py:21
  89.8 328.9 %collective-permute-start.2 = (bf16[1,32,128,256]{3,2,1,0:T(8,128)(2,1)}, bf16[1,32,128,256]{3,2,1,0:T(8,128)(2,1)}, u32[]{:S(2)}, u32[]{:S(2)}) collective-permute-start(bf16[1,32,128,256]{3,2,1,0:T(8,128)(2,1)} %get-tuple-element.84), channel_id=1, source_target_pairs={{0,12},{4,8},{8,4},{12,0},{16,28},{20,24},{24,20},{28,16},{1,13},{... | collective-permute-start | bytes 6291464 | tf_op jit(solution)/shard_map/ppermute | solution.py:21
  89.9 556.2 %collective-permute-start.3 = (bf16[1,32,128,256]{3,2,1,0:T(8,128)(2,1)}, bf16[1,32,128,256]{3,2,1,0:T(8,128)(2,1)}, u32[]{:S(2)}, u32[]{:S(2)}) collective-permute-start(bf16[1,32,128,256]{3,2,1,0:T(8,128)(2,1)} %get-tuple-element.83), channel_id=1, source_target_pairs={{0,16},{4,20},{8,24},{12,28},{16,0},{20,4},{24,8},{28,12},{1,17},{... | collective-permute-start | bytes 6291464 | tf_op jit(solution)/shard_map/ppermute | solution.py:21
  92.7 597.6 %collective-permute-start.4 = (bf16[1,32,128,256]{3,2,1,0:T(8,128)(2,1)}, bf16[1,32,128,256]{3,2,1,0:T(8,128)(2,1)}, u32[]{:S(2)}, u32[]{:S(2)}) collective-permute-start(bf16[1,32,128,256]{3,2,1,0:T(8,128)(2,1)} %get-tuple-element.82), channel_id=1, source_target_pairs={{0,20},{4,16},{8,28},{12,24},{16,4},{20,0},{24,12},{28,8},{1,21},{... | collective-permute-start | bytes 6291464 | tf_op jit(solution)/shard_map/ppermute | solution.py:21
  94.4 7.7 copy-start.6
  115.8 19.4 %copy-start.3 = (bf16[1024,1024]{0,1:T(8,128)(2,1)}, bf16[1024,1024]{0,1:T(8,128)(2,1)S(1)}, u32[]{:S(2)}) copy-start(bf16[1024,1024]{0,1:T(8,128)(2,1)S(1)} %convolution_convert_fusion.1) | copy-start | bytes 6291460
  115.8 19.4 %copy-start.5 = (s32[512]{0:T(512)S(1)}, s32[512]{0:T(512)}, u32[]{:S(2)}) copy-start(s32[512]{0:T(512)} %param.21) | copy-start | bytes 6148
  235.3 458.1 %collective-permute-start.5 = (bf16[1,32,128,256]{3,2,1,0:T(8,128)(2,1)}, bf16[1,32,128,256]{3,2,1,0:T(8,128)(2,1)}, u32[]{:S(2)}, u32[]{:S(2)}) collective-permute-start(bf16[1,32,128,256]{3,2,1,0:T(8,128)(2,1)} %get-tuple-element.81), channel_id=1, source_target_pairs={{0,24},{4,28},{8,16},{12,20},{16,8},{20,12},{24,0},{28,4},{1,25},{... | collective-permute-start | bytes 6291464 | tf_op jit(solution)/shard_map/ppermute | solution.py:21
  373.8 322.9 %collective-permute-start.6 = (bf16[1,32,128,256]{3,2,1,0:T(8,128)(2,1)}, bf16[1,32,128,256]{3,2,1,0:T(8,128)(2,1)S(1)}, u32[]{:S(2)}, u32[]{:S(2)}) collective-permute-start(bf16[1,32,128,256]{3,2,1,0:T(8,128)(2,1)} %get-tuple-element.80), channel_id=1, source_target_pairs={{0,28},{4,24},{8,20},{12,16},{16,12},{20,8},{24,4},{28,0},{1,29},{... | collective-permute-start | bytes 6291464 | tf_op jit(solution)/shard_map/ppermute | solution.py:21
  994.8 4.9 copy-start.7
  994.8 4.9 copy-start.8
  1013.0 166.6 %copy-start.1 = (bf16[4096,256]{1,0:T(8,128)(2,1)S(1)}, bf16[4096,256]{1,0:T(8,128)(2,1)}, u32[]{:S(2)}) copy-start(bf16[4096,256]{1,0:T(8,128)(2,1)} %param.14) | copy-start | bytes 6291460
Sparse Core Ops, SparseCore 0:
  1028.1 151.3 reduce-scatter.1
